TPU v7x, 32 devices: a whole 2x2x4 slice. The times are simulated.
32 devices in a mesh: tm: 4 (over y, x), gx: 8 (over z, core).
Axes of the slice: x: 2, y: 2, z: 4, core: 2. Of those that a mesh axis runs over, the one named last changes fastest.
Arguments:
- state: float32 [8, 32, 256, 128], P('tm', 'gx'), may hold values from -3 to 3
- start_field: float32 [32, 256, 128], P('gx'), may hold values from -3 to 3
- diffusivity: float32 [32, 256, 128], P('gx'), may hold values from 0.3 to 3
- time_weights: float32 [8], P('tm'), may hold values from 0.4 to 1
- shift_real: float32 [8], replicated, may hold values from 0.5 to 2, as said below
- shift_imag: float32 [8], replicated, may hold values from -1 to 1, as said below
Outputs:
- new_state: float32 [8, 32, 256, 128], P('tm', 'gx')
Inputs may be any that keep to these rules, and one draw needn't show every extreme that they name: `shift_real`: shift_real_k = shift_real_(8 - k) for k = 1 .. 7. `shift_imag`: shift_imag_0 = shift_imag_(4) = 0 and shift_imag_k = - shift_imag_(8 - k), so the eigenvalues come in conjugate pairs.
All inputs are finite; a program needn't handle non-finite values.
Results may differ from a plain program's by a relative error of at most 0.0003.
Values sent between devices are 32-bit elements; how exact they have to be, the bound alone decides.
No kernel may reach another device: no remote copies, remote signals or barrier semaphores. Data moves between devices by JAX's collectives and lax.ppermute only.
A program may use at most 64 MiB of HBM per device.

v0:
```python
import math
import jax
import jax.numpy as jnp
from jax import lax
from jax.sharding import PartitionSpec as P

SWEEPS = 12
cheb_centre = 1.0
cheb_half = 0.7


def padded_2(block, sides, width):
    for axis, dim in sides:
        count = lax.axis_size(axis)
        forward = [(i, i + 1) for i in range(count - 1)]
        backward = [(target, source) for source, target in forward]
        low = lax.ppermute(
            lax.slice_in_dim(block, block.shape[dim] - width, None, axis=dim), axis, forward
        )
        high = lax.ppermute(lax.slice_in_dim(block, 0, width, axis=dim), axis, backward)
        block = jnp.concatenate([low, block, high], axis=dim)
    return block


def shifted(value, axis, steps):
    count = lax.axis_size(axis)
    initial, last = (max(0, -steps), min(count, count - steps))
    return lax.ppermute(value, axis, [(source, source + steps) for source in range(initial, last)])


def along(core, axis, lower):
    length = core.shape[axis]
    zeros = jnp.zeros_like(lax.slice_in_dim(core, 0, 1, axis=axis))
    if lower:
        return jnp.concatenate([zeros, lax.slice_in_dim(core, 0, length - 1, axis=axis)], axis)
    return jnp.concatenate([lax.slice_in_dim(core, 1, length, axis=axis), zeros], axis)


def six_near(padded):
    core = padded[..., 1:-1, :, :]
    rank = core.ndim
    return (
        core,
        (
            padded[..., :-2, :, :],
            padded[..., 2:, :, :],
            along(core, rank - 2, True),
            along(core, rank - 2, False),
            along(core, rank - 1, True),
            along(core, rank - 1, False),
        ),
    )


def operate(padded, faces, diag_sum):
    core, near = six_near(padded)
    total = faces[0] * near[0]
    for which in range(1, 6):
        total = total + faces[which] * near[which]
    return diag_sum * core - total


def time_matrix(total_steps, sign):
    index = lax.iota(jnp.int32, total_steps)
    product = index[:, None] * index[None, :] % total_steps
    angle = product.astype(jnp.float32) * (2.0 * math.pi / total_steps)
    cosine = jnp.cos(angle)
    sine = jnp.sin(angle) * sign
    matrix = jnp.stack([jnp.stack([cosine, sine], -1), jnp.stack([-sine, cosine], -1)], 1)
    return matrix.reshape((2 * total_steps, 2 * total_steps))


def apply_time(field, sign):
    total_steps = field.shape[0]
    flat = field.reshape((2 * total_steps, -1))
    mixed = jnp.dot(
        time_matrix(total_steps, sign),
        flat,
        precision=lax.Precision.HIGHEST,
        preferred_element_type=jnp.float32,
    )
    return mixed.reshape(field.shape)


def forward_time(field):
    return apply_time(field, 1.0)


def inverse_time(field):
    return apply_time(field, -1.0)


def shards(state, start_field, diffusivity, time_weights, shift_real, shift_imag):
    local_steps = state.shape[0]
    total_steps = local_steps * lax.axis_size("tm")
    device = lax.axis_index("tm")
    stacked = jnp.concatenate([diffusivity[None], state], 0)
    padded = padded_2(stacked, (("gx", 1),), 1)
    kappa, near = six_near(padded[0])
    faces = [0.5 * (kappa + other) for other in near]
    diag_sum = faces[0]
    for which in range(1, 6):
        diag_sum = diag_sum + faces[which]
    carried = shifted(state[local_steps - 1], "tm", 1)
    first_prior = jnp.where(device == 0, start_field, carried)
    prior = jnp.concatenate([first_prior[None], state[: local_steps - 1]], 0)
    applied = operate(padded[1:], faces, diag_sum)
    residual = prior - state - (applied + state * state * state - state)
    weighted = time_weights[:, None, None, None] * residual
    field = jnp.stack([weighted, jnp.zeros_like(weighted)], 1)
    local_index = device * local_steps + lax.iota(jnp.int32, local_steps)
    spectral = forward_time(lax.all_to_all(field, "tm", split_axis=3, concat_axis=0, tiled=True))
    spectral = lax.all_to_all(spectral, "tm", split_axis=0, concat_axis=3, tiled=True)
    chooser = (local_index[:, None] == lax.iota(jnp.int32, total_steps)[None, :]).astype(
        jnp.float32
    )
    mode_real = jnp.dot(
        chooser, shift_real, precision=lax.Precision.HIGHEST, preferred_element_type=jnp.float32
    ).reshape((-1, 1, 1, 1))
    mode_imag = jnp.dot(
        chooser, shift_imag, precision=lax.Precision.HIGHEST, preferred_element_type=jnp.float32
    ).reshape((-1, 1, 1, 1))
    denom_real = mode_real + diag_sum
    magnitude = denom_real * denom_real + mode_imag * mode_imag
    inverse_real = denom_real / magnitude
    inverse_imag = -mode_imag / magnitude
    source_real = spectral[:, 0]
    source_imag = spectral[:, 1]
    solution = jnp.stack(
        [
            source_real * inverse_real - source_imag * inverse_imag,
            source_real * inverse_imag + source_imag * inverse_real,
        ],
        1,
    )

    def sweep(turn, current):
        omega = 1.0 / (
            cheb_centre
            + cheb_half * jnp.cos(math.pi * (2.0 * turn.astype(jnp.float32) + 1.0) / (2.0 * SWEEPS))
        )
        extended = padded_2(current, (("gx", 2),), 1)
        image = operate(extended, faces, diag_sum)
        answer_real = current[:, 0]
        answer_imag = current[:, 1]
        misfit_real = source_real - (
            mode_real * answer_real - mode_imag * answer_imag + image[:, 0]
        )
        misfit_imag = source_imag - (
            mode_real * answer_imag + mode_imag * answer_real + image[:, 1]
        )
        return jnp.stack(
            [
                answer_real + omega * (misfit_real * inverse_real - misfit_imag * inverse_imag),
                answer_imag + omega * (misfit_real * inverse_imag + misfit_imag * inverse_real),
            ],
            1,
        )

    solution = lax.fori_loop(0, SWEEPS, sweep, solution)
    back = inverse_time(lax.all_to_all(solution, "tm", split_axis=3, concat_axis=0, tiled=True))
    back = lax.all_to_all(back, "tm", split_axis=0, concat_axis=3, tiled=True)
    delta = back[:, 0] / (total_steps * time_weights[:, None, None, None])
    return state + delta


def solution(mesh):
    in_specs = (
        P("tm", "gx", None, None),
        P("gx", None, None),
        P("gx", None, None),
        P("tm"),
        P(),
        P(),
    )
    out_specs = P("tm", "gx", None, None)
    return jax.shard_map(shards, mesh=mesh, in_specs=in_specs, out_specs=out_specs, check_vma=False)
```

profile of v0, /device:TPU:0, one launch (start us, length us, event | category | flops | bytes accessed | tf_op | source)
XLA Modules:
  0.0 402.5 jit_solution(8984971837982444184)
XLA Ops:
  2.4 5.7 %collective-permute-start.2 = (f32[4,256,128]{2,0,1:T(4,128)}, f32[4,256,128]{2,0,1:T(4,128)}, u32[]{:S(2)}, u32[]{:S(2)}) collective-permute-start(f32[4,256,128]{2,0,1:T(4,128)} %bitcast.138), channel_id=1, source_target_pairs={{0,8},{8,16},{16,24},{1,9},{9,17},{17,25},{2,10},{10,18},{18,26},{... | collective-permute-start | bytes 1572872 | tf_op jit(solution)/shard_map/ppermute | solution.py:28
  9.1 1.6 pad_maximum_fusion.11
  16.9 2.3 copy.153
  19.1 2.2 copy.154
  24.4 2.0 multiply_bitcast_fusion.1
  26.4 3.4 add_add_fusion
  30.3 1.6 copy-done.23
  31.9 3.9 fusion.40
  35.8 1.7 stack.76
  37.5 3.8 all-to-all-start
  41.7 24.5 %all-to-all-done = f32[2,2,4,256,128]{4,2,0,1,3:T(4,128)S(1)} async-done(((f32[2,2,4,256,128]{4,2,0,1,3:T(4,128)}), f32[2,2,4,256,128]{4,2,0,1,3:T(4,128)S(1)}, u32[]{:S(2)}, u32[]{:S(2)}) %all-to-all-start) | async-done | bytes 2097184 | tf_op jit(solution)/shard_map/all_to_all | solution.py:112
  66.3 2.0 copy.162
  68.3 1.7 reshape.221
  70.5 2.8 fusion.30
  73.3 1.7 copy.107
  75.0 3.7 all-to-all-start.1
  84.7 20.2 %all-to-all-done.1 = f32[8,2,4,64,128]{4,3,2,1,0:T(8,128)S(1)} async-done(((f32[8,2,4,64,128]{4,3,2,1,0:T(8,128)}), f32[8,2,4,64,128]{4,3,2,1,0:T(8,128)S(1)}, u32[]{:S(2)}, u32[]{:S(2)}) %all-to-all-start.1) | async-done | bytes 2097184 | tf_op jit(solution)/shard_map/all_to_all | solution.py:113
  105.2 1.9 multiply_subtract_fusion
  107.4 222.7 %while.17 = (s32[]{:T(128)}, f32[2,2,4,256,128]{4,3,2,1,0:T(8,128)S(1)}, f32[2,4,256,128]{3,2,1,0:T(8,128)}, f32[2,1,1,1]{0,3,2,1:T(1,128)S(1)}, f32[2,1,1,1]{0,...) while((s32[]{:T(128)}, ...), condition=%wide.region_1.2_spmd.clone.clone, body=%wide.region_0.1_spmd.clone.clone.sunk | while | flops 16252937 | bytes 94683824 | solution.py:160
  109.7 3.8 collective-permute-start.1
  113.6 2.4 fusion.95
  119.0 3.3 fusion.96
  126.2 5.9 %collective-permute-start.1 = (f32[2,2,1,256,128]{4,3,2,1,0:T(8,128)}, f32[2,2,1,256,128]{4,3,2,1,0:T(8,128)}, u32[]{:S(2)}, u32[]{:S(2)}) collective-permute-start(f32[2,2,1,256,128]{4,3,2,1,0:T(8,128)} %get-tuple-element.695), channel_id=1, source_target_pairs={{0,1},{1,2},{2,3},{3,4},{4,5},{5,6},{6,7},{8,9},{9,10},{10,11},{11... | collective-permute-start | bytes 1572872 | tf_op jit(solution)/shard_map/while/body/eval_jaxpr/ppermute | solution.py:17
  132.2 2.4 fusion.95
  137.6 3.3 fusion.96
  144.8 6.1 %collective-permute-start.1 = (f32[2,2,1,256,128]{4,3,2,1,0:T(8,128)}, f32[2,2,1,256,128]{4,3,2,1,0:T(8,128)}, u32[]{:S(2)}, u32[]{:S(2)}) collective-permute-start(f32[2,2,1,256,128]{4,3,2,1,0:T(8,128)} %get-tuple-element.695), channel_id=1, source_target_pairs={{0,1},{1,2},{2,3},{3,4},{4,5},{5,6},{6,7},{8,9},{9,10},{10,11},{11... | collective-permute-start | bytes 1572872 | tf_op jit(solution)/shard_map/while/body/eval_jaxpr/ppermute | solution.py:17
  150.9 2.4 fusion.95
  156.3 3.3 fusion.96
  163.6 6.1 %collective-permute-start.1 = (f32[2,2,1,256,128]{4,3,2,1,0:T(8,128)}, f32[2,2,1,256,128]{4,3,2,1,0:T(8,128)}, u32[]{:S(2)}, u32[]{:S(2)}) collective-permute-start(f32[2,2,1,256,128]{4,3,2,1,0:T(8,128)} %get-tuple-element.695), channel_id=1, source_target_pairs={{0,1},{1,2},{2,3},{3,4},{4,5},{5,6},{6,7},{8,9},{9,10},{10,11},{11... | collective-permute-start | bytes 1572872 | tf_op jit(solution)/shard_map/while/body/eval_jaxpr/ppermute | solution.py:17
  169.7 2.4 fusion.95
  175.1 3.3 fusion.96
  182.3 6.1 %collective-permute-start.1 = (f32[2,2,1,256,128]{4,3,2,1,0:T(8,128)}, f32[2,2,1,256,128]{4,3,2,1,0:T(8,128)}, u32[]{:S(2)}, u32[]{:S(2)}) collective-permute-start(f32[2,2,1,256,128]{4,3,2,1,0:T(8,128)} %get-tuple-element.695), channel_id=1, source_target_pairs={{0,1},{1,2},{2,3},{3,4},{4,5},{5,6},{6,7},{8,9},{9,10},{10,11},{11... | collective-permute-start | bytes 1572872 | tf_op jit(solution)/shard_map/while/body/eval_jaxpr/ppermute | solution.py:17
  188.4 2.4 fusion.95
  193.9 3.3 fusion.96
  201.1 6.1 %collective-permute-start.1 = (f32[2,2,1,256,128]{4,3,2,1,0:T(8,128)}, f32[2,2,1,256,128]{4,3,2,1,0:T(8,128)}, u32[]{:S(2)}, u32[]{:S(2)}) collective-permute-start(f32[2,2,1,256,128]{4,3,2,1,0:T(8,128)} %get-tuple-element.695), channel_id=1, source_target_pairs={{0,1},{1,2},{2,3},{3,4},{4,5},{5,6},{6,7},{8,9},{9,10},{10,11},{11... | collective-permute-start | bytes 1572872 | tf_op jit(solution)/shard_map/while/body/eval_jaxpr/ppermute | solution.py:17
  207.2 2.4 fusion.95
  212.6 3.3 fusion.96
  219.9 6.1 %collective-permute-start.1 = (f32[2,2,1,256,128]{4,3,2,1,0:T(8,128)}, f32[2,2,1,256,128]{4,3,2,1,0:T(8,128)}, u32[]{:S(2)}, u32[]{:S(2)}) collective-permute-start(f32[2,2,1,256,128]{4,3,2,1,0:T(8,128)} %get-tuple-element.695), channel_id=1, source_target_pairs={{0,1},{1,2},{2,3},{3,4},{4,5},{5,6},{6,7},{8,9},{9,10},{10,11},{11... | collective-permute-start | bytes 1572872 | tf_op jit(solution)/shard_map/while/body/eval_jaxpr/ppermute | solution.py:17
  226.0 2.4 fusion.95
  231.4 3.3 fusion.96
  238.6 6.1 %collective-permute-start.1 = (f32[2,2,1,256,128]{4,3,2,1,0:T(8,128)}, f32[2,2,1,256,128]{4,3,2,1,0:T(8,128)}, u32[]{:S(2)}, u32[]{:S(2)}) collective-permute-start(f32[2,2,1,256,128]{4,3,2,1,0:T(8,128)} %get-tuple-element.695), channel_id=1, source_target_pairs={{0,1},{1,2},{2,3},{3,4},{4,5},{5,6},{6,7},{8,9},{9,10},{10,11},{11... | collective-permute-start | bytes 1572872 | tf_op jit(solution)/shard_map/while/body/eval_jaxpr/ppermute | solution.py:17
  244.7 2.4 fusion.95
  250.2 3.3 fusion.96
  257.4 6.1 %collective-permute-start.1 = (f32[2,2,1,256,128]{4,3,2,1,0:T(8,128)}, f32[2,2,1,256,128]{4,3,2,1,0:T(8,128)}, u32[]{:S(2)}, u32[]{:S(2)}) collective-permute-start(f32[2,2,1,256,128]{4,3,2,1,0:T(8,128)} %get-tuple-element.695), channel_id=1, source_target_pairs={{0,1},{1,2},{2,3},{3,4},{4,5},{5,6},{6,7},{8,9},{9,10},{10,11},{11... | collective-permute-start | bytes 1572872 | tf_op jit(solution)/shard_map/while/body/eval_jaxpr/ppermute | solution.py:17
  263.5 2.4 fusion.95
  268.9 3.3 fusion.96
  276.1 6.1 %collective-permute-start.1 = (f32[2,2,1,256,128]{4,3,2,1,0:T(8,128)}, f32[2,2,1,256,128]{4,3,2,1,0:T(8,128)}, u32[]{:S(2)}, u32[]{:S(2)}) collective-permute-start(f32[2,2,1,256,128]{4,3,2,1,0:T(8,128)} %get-tuple-element.695), channel_id=1, source_target_pairs={{0,1},{1,2},{2,3},{3,4},{4,5},{5,6},{6,7},{8,9},{9,10},{10,11},{11... | collective-permute-start | bytes 1572872 | tf_op jit(solution)/shard_map/while/body/eval_jaxpr/ppermute | solution.py:17
  282.3 2.4 fusion.95
  287.7 3.3 fusion.96
  294.9 6.1 %collective-permute-start.1 = (f32[2,2,1,256,128]{4,3,2,1,0:T(8,128)}, f32[2,2,1,256,128]{4,3,2,1,0:T(8,128)}, u32[]{:S(2)}, u32[]{:S(2)}) collective-permute-start(f32[2,2,1,256,128]{4,3,2,1,0:T(8,128)} %get-tuple-element.695), channel_id=1, source_target_pairs={{0,1},{1,2},{2,3},{3,4},{4,5},{5,6},{6,7},{8,9},{9,10},{10,11},{11... | collective-permute-start | bytes 1572872 | tf_op jit(solution)/shard_map/while/body/eval_jaxpr/ppermute | solution.py:17
  301.0 2.4 fusion.95
  306.4 3.3 fusion.96
  313.7 6.1 %collective-permute-start.1 = (f32[2,2,1,256,128]{4,3,2,1,0:T(8,128)}, f32[2,2,1,256,128]{4,3,2,1,0:T(8,128)}, u32[]{:S(2)}, u32[]{:S(2)}) collective-permute-start(f32[2,2,1,256,128]{4,3,2,1,0:T(8,128)} %get-tuple-element.695), channel_id=1, source_target_pairs={{0,1},{1,2},{2,3},{3,4},{4,5},{5,6},{6,7},{8,9},{9,10},{10,11},{11... | collective-permute-start | bytes 1572872 | tf_op jit(solution)/shard_map/while/body/eval_jaxpr/ppermute | solution.py:17
  319.8 2.4 fusion.95
  325.2 3.3 fusion.96
  330.1 2.7 copy.118
  332.8 3.8 all-to-all-start.2
  336.9 24.7 %all-to-all-done.2 = f32[2,2,4,256,128]{4,2,1,0,3:T(4,128)S(1)} async-done(((f32[2,2,4,256,128]{4,2,1,0,3:T(4,128)}), f32[2,2,4,256,128]{4,2,1,0,3:T(4,128)S(1)}, u32[]{:S(2)}, u32[]{:S(2)}) %all-to-all-start.2) | async-done | bytes 2097184 | tf_op jit(solution)/shard_map/all_to_all | solution.py:161
  361.6 2.0 copy.161
  363.6 1.7 reshape.224
  365.7 2.8 fusion.28
  368.6 1.7 copy.121
  370.3 3.6 all-to-all-start.3
  373.9 26.1 %all-to-all-done.3 = f32[8,2,4,64,128]{4,3,2,1,0:T(8,128)S(1)} async-done(((f32[8,2,4,64,128]{4,3,2,1,0:T(8,128)}), f32[8,2,4,64,128]{4,3,2,1,0:T(8,128)S(1)}, u32[]{:S(2)}, u32[]{:S(2)}) %all-to-all-start.3) | async-done | bytes 2097184 | tf_op jit(solution)/shard_map/all_to_all | solution.py:162
  (409 shorter events, 103.5 us)
Async XLA Ops:
  0.0 79.0 %copy-start = (f32[8]{0:T(128)S(1)}, f32[8]{0:T(128)}, u32[]{:S(2)}) copy-start(f32[8]{0:T(128)} %param.13) | copy-start | bytes 100
  0.0 8.0 %copy-start.12 = (f32[2,4,256,128]{3,2,1,0:T(8,128)S(1)}, f32[2,4,256,128]{3,2,1,0:T(8,128)}, u32[]{:S(2)}) copy-start(f32[2,4,256,128]{3,2,1,0:T(8,128)} %param.8) | copy-start | bytes 3145732
  0.0 8.7 %copy-start.6 = (f32[4,256,128]{2,1,0:T(8,128)S(1)}, f32[4,256,128]{2,1,0:T(8,128)}, u32[]{:S(2)}) copy-start(f32[4,256,128]{2,1,0:T(8,128)} %param.10) | copy-start | bytes 1572868
  2.4 27.5 %collective-permute-start.2 = (f32[4,256,128]{2,0,1:T(4,128)}, f32[4,256,128]{2,0,1:T(4,128)}, u32[]{:S(2)}, u32[]{:S(2)}) collective-permute-start(f32[4,256,128]{2,0,1:T(4,128)} %bitcast.138), channel_id=1, source_target_pairs={{0,8},{8,16},{16,24},{1,9},{9,17},{17,25},{2,10},{10,18},{18,26},{... | collective-permute-start | bytes 1572872 | tf_op jit(solution)/shard_map/ppermute | solution.py:28
  10.6 13.7 %collective-permute-start.3 = (f32[3,1,256,128]{3,1,0,2:T(1,128)}, f32[3,1,256,128]{3,1,0,2:T(1,128)S(1)}, u32[]{:S(2)}, u32[]{:S(2)}) collective-permute-start(f32[3,1,256,128]{3,1,0,2:T(1,128)} %get-tuple-element.566), channel_id=1, source_target_pairs={{0,1},{1,2},{2,3},{3,4},{4,5},{5,6},{6,7},{8,9},{9,10},{10,11},{11... | collective-permute-start | bytes 1179656 | tf_op jit(solution)/shard_map/ppermute | solution.py:17
  12.1 12.2 %collective-permute-start.4 = (f32[3,1,256,128]{3,1,0,2:T(1,128)}, f32[3,1,256,128]{3,1,0,2:T(1,128)}, u32[]{:S(2)}, u32[]{:S(2)}) collective-permute-start(f32[3,1,256,128]{3,1,0,2:T(1,128)} %get-tuple-element.567), channel_id=1, source_target_pairs={{1,0},{2,1},{3,2},{4,3},{5,4},{6,5},{7,6},{9,8},{10,9},{11,10},{12... | collective-permute-start | bytes 1179656 | tf_op jit(solution)/shard_map/ppermute | solution.py:20
  16.9 4.5 %copy-start.29 = (f32[4,256,127]{2,1,0:T(8,128)S(1)}, f32[4,256,127]{2,1,0:T(8,128)}, u32[]{:S(2)}) copy-start(f32[4,256,127]{2,1,0:T(8,128)} %get-tuple-element.573) | copy-start | bytes 1560580
  16.9 5.6 %copy-start.28 = (f32[4,256,127]{2,1,0:T(8,128)S(1)}, f32[4,256,127]{2,1,0:T(8,128)}, u32[]{:S(2)}) copy-start(f32[4,256,127]{2,1,0:T(8,128)} %get-tuple-element.574) | copy-start | bytes 1560580
  26.4 3.5 copy-start.32
  26.4 3.9 copy-start.33
  29.8 5.9 %copy-start.14 = (f32[4,256,128]{2,0,1:T(4,128)}, f32[4,256,128]{2,0,1:T(4,128)S(1)}, u32[]{:S(2)}) copy-start(f32[4,256,128]{2,0,1:T(4,128)S(1)} %get-tuple-element.553) | copy-start | bytes 1572868
  29.8 6.0 %copy-start.16 = (f32[4,256,128]{2,0,1:T(4,128)}, f32[4,256,128]{2,0,1:T(4,128)S(1)}, u32[]{:S(2)}) copy-start(f32[4,256,128]{2,0,1:T(4,128)S(1)} %get-tuple-element.552) | copy-start | bytes 1572868
  29.8 6.0 %copy-start.18 = (f32[4,256,128]{2,0,1:T(4,128)}, f32[4,256,128]{2,0,1:T(4,128)S(1)}, u32[]{:S(2)}) copy-start(f32[4,256,128]{2,0,1:T(4,128)S(1)} %get-tuple-element.551) | copy-start | bytes 1572868
  29.8 6.0 %copy-start.20 = (f32[4,256,128]{2,0,1:T(4,128)}, f32[4,256,128]{2,0,1:T(4,128)S(1)}, u32[]{:S(2)}) copy-start(f32[4,256,128]{2,0,1:T(4,128)S(1)} %get-tuple-element.550) | copy-start | bytes 1572868
  29.8 6.0 %copy-start.21 = (f32[4,256,128]{2,0,1:T(4,128)}, f32[4,256,128]{2,0,1:T(4,128)S(1)}, u32[]{:S(2)}) copy-start(f32[4,256,128]{2,0,1:T(4,128)S(1)} %get-tuple-element.547) | copy-start | bytes 1572868
  37.5 28.8 %all-to-all-start = ((f32[2,2,4,256,128]{4,2,0,1,3:T(4,128)}), f32[2,2,4,256,128]{4,2,0,1,3:T(4,128)S(1)}, u32[]{:S(2)}, u32[]{:S(2)}) async-start(f32[2,2,4,256,128]{4,2,0,1,3:T(4,128)} %stack.76), calls=%async_computation | async-start | bytes 4194304 | tf_op jit(solution)/shard_map/all_to_all | solution.py:112
  75.0 3.8 copy-start.34
  75.0 4.2 %copy-start.22 = (f32[4,256,128]{2,0,1:T(4,128)S(1)}, f32[4,256,128]{2,0,1:T(4,128)}, u32[]{:S(2)}) copy-start(f32[4,256,128]{2,0,1:T(4,128)} %copy-done.21) | copy-start | bytes 1572868
  75.0 29.9 %all-to-all-start.1 = ((f32[8,2,4,64,128]{4,3,2,1,0:T(8,128)}), f32[8,2,4,64,128]{4,3,2,1,0:T(8,128)S(1)}, u32[]{:S(2)}, u32[]{:S(2)}) async-start(f32[8,2,4,64,128]{4,3,2,1,0:T(8,128)} %copy.107), calls=%async_computation.1 | async-start | bytes 4194304 | tf_op jit(solution)/shard_map/all_to_all | solution.py:113
  79.3 3.7 copy-start.25
  80.4 3.4 copy-start.24
  108.5 8.4 %collective-permute-start = (f32[2,2,1,256,128]{4,3,2,1,0:T(8,128)}, f32[2,2,1,256,128]{4,3,2,1,0:T(8,128)}, u32[]{:S(2)}, u32[]{:S(2)}) collective-permute-start(f32[2,2,1,256,128]{4,3,2,1,0:T(8,128)} %get-tuple-element.694), channel_id=1, source_target_pairs={{1,0},{2,1},{3,2},{4,3},{5,4},{6,5},{7,6},{9,8},{10,9},{11,10},{12... | collective-permute-start | bytes 1572872 | tf_op jit(solution)/shard_map/while/body/eval_jaxpr/ppermute | solution.py:20
  109.7 7.1 %collective-permute-start.1 = (f32[2,2,1,256,128]{4,3,2,1,0:T(8,128)}, f32[2,2,1,256,128]{4,3,2,1,0:T(8,128)}, u32[]{:S(2)}, u32[]{:S(2)}) collective-permute-start(f32[2,2,1,256,128]{4,3,2,1,0:T(8,128)} %get-tuple-element.695), channel_id=1, source_target_pairs={{0,1},{1,2},{2,3},{3,4},{4,5},{5,6},{6,7},{8,9},{9,10},{10,11},{11... | collective-permute-start | bytes 1572872 | tf_op jit(solution)/shard_map/while/body/eval_jaxpr/ppermute | solution.py:17
  119.0 3.4 copy-start.4
  119.0 3.4 copy-start.5
  124.9 10.5 %collective-permute-start = (f32[2,2,1,256,128]{4,3,2,1,0:T(8,128)}, f32[2,2,1,256,128]{4,3,2,1,0:T(8,128)}, u32[]{:S(2)}, u32[]{:S(2)}) collective-permute-start(f32[2,2,1,256,128]{4,3,2,1,0:T(8,128)} %get-tuple-element.694), channel_id=1, source_target_pairs={{1,0},{2,1},{3,2},{4,3},{5,4},{6,5},{7,6},{9,8},{10,9},{11,10},{12... | collective-permute-start | bytes 1572872 | tf_op jit(solution)/shard_map/while/body/eval_jaxpr/ppermute | solution.py:20
  126.2 9.2 %collective-permute-start.1 = (f32[2,2,1,256,128]{4,3,2,1,0:T(8,128)}, f32[2,2,1,256,128]{4,3,2,1,0:T(8,128)}, u32[]{:S(2)}, u32[]{:S(2)}) collective-permute-start(f32[2,2,1,256,128]{4,3,2,1,0:T(8,128)} %get-tuple-element.695), channel_id=1, source_target_pairs={{0,1},{1,2},{2,3},{3,4},{4,5},{5,6},{6,7},{8,9},{9,10},{10,11},{11... | collective-permute-start | bytes 1572872 | tf_op jit(solution)/shard_map/while/body/eval_jaxpr/ppermute | solution.py:17
  137.6 3.4 copy-start.4
  137.6 3.4 copy-start.5
  143.5 10.7 %collective-permute-start = (f32[2,2,1,256,128]{4,3,2,1,0:T(8,128)}, f32[2,2,1,256,128]{4,3,2,1,0:T(8,128)}, u32[]{:S(2)}, u32[]{:S(2)}) collective-permute-start(f32[2,2,1,256,128]{4,3,2,1,0:T(8,128)} %get-tuple-element.694), channel_id=1, source_target_pairs={{1,0},{2,1},{3,2},{4,3},{5,4},{6,5},{7,6},{9,8},{10,9},{11,10},{12... | collective-permute-start | bytes 1572872 | tf_op jit(solution)/shard_map/while/body/eval_jaxpr/ppermute | solution.py:20
  144.8 9.4 %collective-permute-start.1 = (f32[2,2,1,256,128]{4,3,2,1,0:T(8,128)}, f32[2,2,1,256,128]{4,3,2,1,0:T(8,128)}, u32[]{:S(2)}, u32[]{:S(2)}) collective-permute-start(f32[2,2,1,256,128]{4,3,2,1,0:T(8,128)} %get-tuple-element.695), channel_id=1, source_target_pairs={{0,1},{1,2},{2,3},{3,4},{4,5},{5,6},{6,7},{8,9},{9,10},{10,11},{11... | collective-permute-start | bytes 1572872 | tf_op jit(solution)/shard_map/while/body/eval_jaxpr/ppermute | solution.py:17
  156.3 3.4 copy-start.4
  156.3 3.4 copy-start.5
  162.3 10.7 %collective-permute-start = (f32[2,2,1,256,128]{4,3,2,1,0:T(8,128)}, f32[2,2,1,256,128]{4,3,2,1,0:T(8,128)}, u32[]{:S(2)}, u32[]{:S(2)}) collective-permute-start(f32[2,2,1,256,128]{4,3,2,1,0:T(8,128)} %get-tuple-element.694), channel_id=1, source_target_pairs={{1,0},{2,1},{3,2},{4,3},{5,4},{6,5},{7,6},{9,8},{10,9},{11,10},{12... | collective-permute-start | bytes 1572872 | tf_op jit(solution)/shard_map/while/body/eval_jaxpr/ppermute | solution.py:20
  163.6 9.4 %collective-permute-start.1 = (f32[2,2,1,256,128]{4,3,2,1,0:T(8,128)}, f32[2,2,1,256,128]{4,3,2,1,0:T(8,128)}, u32[]{:S(2)}, u32[]{:S(2)}) collective-permute-start(f32[2,2,1,256,128]{4,3,2,1,0:T(8,128)} %get-tuple-element.695), channel_id=1, source_target_pairs={{0,1},{1,2},{2,3},{3,4},{4,5},{5,6},{6,7},{8,9},{9,10},{10,11},{11... | collective-permute-start | bytes 1572872 | tf_op jit(solution)/shard_map/while/body/eval_jaxpr/ppermute | solution.py:17
  175.1 3.4 copy-start.5
  181.0 10.7 %collective-permute-start = (f32[2,2,1,256,128]{4,3,2,1,0:T(8,128)}, f32[2,2,1,256,128]{4,3,2,1,0:T(8,128)}, u32[]{:S(2)}, u32[]{:S(2)}) collective-permute-start(f32[2,2,1,256,128]{4,3,2,1,0:T(8,128)} %get-tuple-element.694), channel_id=1, source_target_pairs={{1,0},{2,1},{3,2},{4,3},{5,4},{6,5},{7,6},{9,8},{10,9},{11,10},{12... | collective-permute-start | bytes 1572872 | tf_op jit(solution)/shard_map/while/body/eval_jaxpr/ppermute | solution.py:20
  182.3 9.4 %collective-permute-start.1 = (f32[2,2,1,256,128]{4,3,2,1,0:T(8,128)}, f32[2,2,1,256,128]{4,3,2,1,0:T(8,128)}, u32[]{:S(2)}, u32[]{:S(2)}) collective-permute-start(f32[2,2,1,256,128]{4,3,2,1,0:T(8,128)} %get-tuple-element.695), channel_id=1, source_target_pairs={{0,1},{1,2},{2,3},{3,4},{4,5},{5,6},{6,7},{8,9},{9,10},{10,11},{11... | collective-permute-start | bytes 1572872 | tf_op jit(solution)/shard_map/while/body/eval_jaxpr/ppermute | solution.py:17
  193.9 3.4 copy-start.4
  193.9 3.4 copy-start.5
  199.8 10.7 %collective-permute-start = (f32[2,2,1,256,128]{4,3,2,1,0:T(8,128)}, f32[2,2,1,256,128]{4,3,2,1,0:T(8,128)}, u32[]{:S(2)}, u32[]{:S(2)}) collective-permute-start(f32[2,2,1,256,128]{4,3,2,1,0:T(8,128)} %get-tuple-element.694), channel_id=1, source_target_pairs={{1,0},{2,1},{3,2},{4,3},{5,4},{6,5},{7,6},{9,8},{10,9},{11,10},{12... | collective-permute-start | bytes 1572872 | tf_op jit(solution)/shard_map/while/body/eval_jaxpr/ppermute | solution.py:20
  201.1 9.4 %collective-permute-start.1 = (f32[2,2,1,256,128]{4,3,2,1,0:T(8,128)}, f32[2,2,1,256,128]{4,3,2,1,0:T(8,128)}, u32[]{:S(2)}, u32[]{:S(2)}) collective-permute-start(f32[2,2,1,256,128]{4,3,2,1,0:T(8,128)} %get-tuple-element.695), channel_id=1, source_target_pairs={{0,1},{1,2},{2,3},{3,4},{4,5},{5,6},{6,7},{8,9},{9,10},{10,11},{11... | collective-permute-start | bytes 1572872 | tf_op jit(solution)/shard_map/while/body/eval_jaxpr/ppermute | solution.py:17
  212.6 3.4 copy-start.4
  212.6 3.4 copy-start.5
  218.6 10.7 %collective-permute-start = (f32[2,2,1,256,128]{4,3,2,1,0:T(8,128)}, f32[2,2,1,256,128]{4,3,2,1,0:T(8,128)}, u32[]{:S(2)}, u32[]{:S(2)}) collective-permute-start(f32[2,2,1,256,128]{4,3,2,1,0:T(8,128)} %get-tuple-element.694), channel_id=1, source_target_pairs={{1,0},{2,1},{3,2},{4,3},{5,4},{6,5},{7,6},{9,8},{10,9},{11,10},{12... | collective-permute-start | bytes 1572872 | tf_op jit(solution)/shard_map/while/body/eval_jaxpr/ppermute | solution.py:20
  219.9 9.4 %collective-permute-start.1 = (f32[2,2,1,256,128]{4,3,2,1,0:T(8,128)}, f32[2,2,1,256,128]{4,3,2,1,0:T(8,128)}, u32[]{:S(2)}, u32[]{:S(2)}) collective-permute-start(f32[2,2,1,256,128]{4,3,2,1,0:T(8,128)} %get-tuple-element.695), channel_id=1, source_target_pairs={{0,1},{1,2},{2,3},{3,4},{4,5},{5,6},{6,7},{8,9},{9,10},{10,11},{11... | collective-permute-start | bytes 1572872 | tf_op jit(solution)/shard_map/while/body/eval_jaxpr/ppermute | solution.py:17
  231.4 3.4 copy-start.5
  237.3 10.7 %collective-permute-start = (f32[2,2,1,256,128]{4,3,2,1,0:T(8,128)}, f32[2,2,1,256,128]{4,3,2,1,0:T(8,128)}, u32[]{:S(2)}, u32[]{:S(2)}) collective-permute-start(f32[2,2,1,256,128]{4,3,2,1,0:T(8,128)} %get-tuple-element.694), channel_id=1, source_target_pairs={{1,0},{2,1},{3,2},{4,3},{5,4},{6,5},{7,6},{9,8},{10,9},{11,10},{12... | collective-permute-start | bytes 1572872 | tf_op jit(solution)/shard_map/while/body/eval_jaxpr/ppermute | solution.py:20
  238.6 9.4 %collective-permute-start.1 = (f32[2,2,1,256,128]{4,3,2,1,0:T(8,128)}, f32[2,2,1,256,128]{4,3,2,1,0:T(8,128)}, u32[]{:S(2)}, u32[]{:S(2)}) collective-permute-start(f32[2,2,1,256,128]{4,3,2,1,0:T(8,128)} %get-tuple-element.695), channel_id=1, source_target_pairs={{0,1},{1,2},{2,3},{3,4},{4,5},{5,6},{6,7},{8,9},{9,10},{10,11},{11... | collective-permute-start | bytes 1572872 | tf_op jit(solution)/shard_map/while/body/eval_jaxpr/ppermute | solution.py:17
  250.1 3.4 copy-start.5
  256.1 10.7 %collective-permute-start = (f32[2,2,1,256,128]{4,3,2,1,0:T(8,128)}, f32[2,2,1,256,128]{4,3,2,1,0:T(8,128)}, u32[]{:S(2)}, u32[]{:S(2)}) collective-permute-start(f32[2,2,1,256,128]{4,3,2,1,0:T(8,128)} %get-tuple-element.694), channel_id=1, source_target_pairs={{1,0},{2,1},{3,2},{4,3},{5,4},{6,5},{7,6},{9,8},{10,9},{11,10},{12... | collective-permute-start | bytes 1572872 | tf_op jit(solution)/shard_map/while/body/eval_jaxpr/ppermute | solution.py:20
  257.4 9.4 %collective-permute-start.1 = (f32[2,2,1,256,128]{4,3,2,1,0:T(8,128)}, f32[2,2,1,256,128]{4,3,2,1,0:T(8,128)}, u32[]{:S(2)}, u32[]{:S(2)}) collective-permute-start(f32[2,2,1,256,128]{4,3,2,1,0:T(8,128)} %get-tuple-element.695), channel_id=1, source_target_pairs={{0,1},{1,2},{2,3},{3,4},{4,5},{5,6},{6,7},{8,9},{9,10},{10,11},{11... | collective-permute-start | bytes 1572872 | tf_op jit(solution)/shard_map/while/body/eval_jaxpr/ppermute | solution.py:17
  268.9 3.4 copy-start.5
  274.9 10.7 %collective-permute-start = (f32[2,2,1,256,128]{4,3,2,1,0:T(8,128)}, f32[2,2,1,256,128]{4,3,2,1,0:T(8,128)}, u32[]{:S(2)}, u32[]{:S(2)}) collective-permute-start(f32[2,2,1,256,128]{4,3,2,1,0:T(8,128)} %get-tuple-element.694), channel_id=1, source_target_pairs={{1,0},{2,1},{3,2},{4,3},{5,4},{6,5},{7,6},{9,8},{10,9},{11,10},{12... | collective-permute-start | bytes 1572872 | tf_op jit(solution)/shard_map/while/body/eval_jaxpr/ppermute | solution.py:20
  276.1 9.4 %collective-permute-start.1 = (f32[2,2,1,256,128]{4,3,2,1,0:T(8,128)}, f32[2,2,1,256,128]{4,3,2,1,0:T(8,128)}, u32[]{:S(2)}, u32[]{:S(2)}) collective-permute-start(f32[2,2,1,256,128]{4,3,2,1,0:T(8,128)} %get-tuple-element.695), channel_id=1, source_target_pairs={{0,1},{1,2},{2,3},{3,4},{4,5},{5,6},{6,7},{8,9},{9,10},{10,11},{11... | collective-permute-start | bytes 1572872 | tf_op jit(solution)/shard_map/while/body/eval_jaxpr/ppermute | solution.py:17
  287.7 3.4 copy-start.5
  293.6 10.7 %collective-permute-start = (f32[2,2,1,256,128]{4,3,2,1,0:T(8,128)}, f32[2,2,1,256,128]{4,3,2,1,0:T(8,128)}, u32[]{:S(2)}, u32[]{:S(2)}) collective-permute-start(f32[2,2,1,256,128]{4,3,2,1,0:T(8,128)} %get-tuple-element.694), channel_id=1, source_target_pairs={{1,0},{2,1},{3,2},{4,3},{5,4},{6,5},{7,6},{9,8},{10,9},{11,10},{12... | collective-permute-start | bytes 1572872 | tf_op jit(solution)/shard_map/while/body/eval_jaxpr/ppermute | solution.py:20
  294.9 9.4 %collective-permute-start.1 = (f32[2,2,1,256,128]{4,3,2,1,0:T(8,128)}, f32[2,2,1,256,128]{4,3,2,1,0:T(8,128)}, u32[]{:S(2)}, u32[]{:S(2)}) collective-permute-start(f32[2,2,1,256,128]{4,3,2,1,0:T(8,128)} %get-tuple-element.695), channel_id=1, source_target_pairs={{0,1},{1,2},{2,3},{3,4},{4,5},{5,6},{6,7},{8,9},{9,10},{10,11},{11... | collective-permute-start | bytes 1572872 | tf_op jit(solution)/shard_map/while/body/eval_jaxpr/ppermute | solution.py:17
  306.4 3.4 copy-start.5
  312.4 10.7 %collective-permute-start = (f32[2,2,1,256,128]{4,3,2,1,0:T(8,128)}, f32[2,2,1,256,128]{4,3,2,1,0:T(8,128)}, u32[]{:S(2)}, u32[]{:S(2)}) collective-permute-start(f32[2,2,1,256,128]{4,3,2,1,0:T(8,128)} %get-tuple-element.694), channel_id=1, source_target_pairs={{1,0},{2,1},{3,2},{4,3},{5,4},{6,5},{7,6},{9,8},{10,9},{11,10},{12... | collective-permute-start | bytes 1572872 | tf_op jit(solution)/shard_map/while/body/eval_jaxpr/ppermute | solution.py:20
  313.7 9.4 %collective-permute-start.1 = (f32[2,2,1,256,128]{4,3,2,1,0:T(8,128)}, f32[2,2,1,256,128]{4,3,2,1,0:T(8,128)}, u32[]{:S(2)}, u32[]{:S(2)}) collective-permute-start(f32[2,2,1,256,128]{4,3,2,1,0:T(8,128)} %get-tuple-element.695), channel_id=1, source_target_pairs={{0,1},{1,2},{2,3},{3,4},{4,5},{5,6},{6,7},{8,9},{9,10},{10,11},{11... | collective-permute-start | bytes 1572872 | tf_op jit(solution)/shard_map/while/body/eval_jaxpr/ppermute | solution.py:17
  325.2 3.4 copy-start.5
  332.8 28.8 %all-to-all-start.2 = ((f32[2,2,4,256,128]{4,2,1,0,3:T(4,128)}), f32[2,2,4,256,128]{4,2,1,0,3:T(4,128)S(1)}, u32[]{:S(2)}, u32[]{:S(2)}) async-start(f32[2,2,4,256,128]{4,2,1,0,3:T(4,128)} %copy.118), calls=%async_computation.2 | async-start | bytes 4194304 | tf_op jit(solution)/shard_map/all_to_all | solution.py:161
  370.3 29.8 %all-to-all-start.3 = ((f32[8,2,4,64,128]{4,3,2,1,0:T(8,128)}), f32[8,2,4,64,128]{4,3,2,1,0:T(8,128)S(1)}, u32[]{:S(2)}, u32[]{:S(2)}) async-start(f32[8,2,4,64,128]{4,3,2,1,0:T(8,128)} %copy.121), calls=%async_computation.3 | async-start | bytes 4194304 | tf_op jit(solution)/shard_map/all_to_all | solution.py:162
  (101 other events, 244.5 us)
where the time goes:
time: 404 us; the launch traced here: 402 us
  local copies, waits for them, and re-layouts  115 us (28%)
  starting transfers between devices  110 us (27%)
  waiting for transfers between devices  95.7 us (24%)
  other arithmetic  72.4 us (18%)
  matrix products  6.04 us (1%)
    ppermute x13, starting transfers between devices, padded_2(): lax.ppermute(lax.slice_in_dim(block, block.shape[dim] - width, None, axis...  72.5 us
    sub x12, other arithmetic, operate(): return diag_sum * core - total  40.2 us
    slice x26, local copies, waits for them, and re-layouts, along(): lax.slice_in_dim(core, 0, length - 1, axis=axis)  38.9 us
    all_to_all x1, waiting for transfers between devices, shards(): back = lax.all_to_all(back, 'tm', split_axis=0, concat_axis=3, tiled=True)  26.1 us
    while x216, local copies, waits for them, and re-layouts  25.5 us
    all_to_all x1, waiting for transfers between devices, shards(): lax.all_to_all(solution, 'tm', split_axis=3, concat_axis=0, tiled=True)  24.7 us
    all_to_all x1, waiting for transfers between devices, shards(): lax.all_to_all(field, 'tm', split_axis=3, concat_axis=0, tiled=True)  24.5 us
    all_to_all x1, waiting for transfers between devices, shards(): lax.all_to_all(spectral, 'tm', split_axis=0, concat_axis=3, tiled=True)  20.2 us
  transfers between devices with their start and end apart: 31, of which 4 were waited for; matrix products, arithmetic and copies ran while one was open for 15% of the time, Pallas kernels for 0%

commit v1 on v0

--- a/solution.py
+++ b/solution.py
@@ -110,7 +110,10 @@
     field = jnp.stack([weighted, jnp.zeros_like(weighted)], 1)
     local_index = device * local_steps + lax.iota(jnp.int32, local_steps)
     spectral = forward_time(lax.all_to_all(field, "tm", split_axis=3, concat_axis=0, tiled=True))
-    spectral = lax.all_to_all(spectral, "tm", split_axis=0, concat_axis=3, tiled=True)
+    spectral = jnp.concatenate(
+        lax.all_to_all(jnp.stack(jnp.split(spectral, lax.axis_size("tm"), axis=0)), "tm", 0, 0),
+        axis=3,
+    )
     chooser = (local_index[:, None] == lax.iota(jnp.int32, total_steps)[None, :]).astype(
         jnp.float32
     )

time: 404 us -> 403 us (level)
    unnamed x68 -> x72, local copies, waits for them, and re-layouts: 17.9 us -> 17.9 us
where the time goes in v1:
time: 403 us; the launch traced here: 401 us
  local copies, waits for them, and re-layouts  113 us (28%)
  starting transfers between devices  110 us (27%)
  waiting for transfers between devices  95.7 us (24%)
  other arithmetic  73.8 us (18%)
  matrix products  5.1 us (1%)
    ppermute x13, starting transfers between devices, padded_2(): lax.ppermute(lax.slice_in_dim(block, block.shape[dim] - width, None, axis...  72.5 us
    sub x12, other arithmetic, operate(): return diag_sum * core - total  40.2 us
    slice x26, local copies, waits for them, and re-layouts, along(): lax.slice_in_dim(core, 0, length - 1, axis=axis)  38.8 us
    all_to_all x1, waiting for transfers between devices, shards(): back = lax.all_to_all(back, 'tm', split_axis=0, concat_axis=3, tiled=True)  26.1 us
    while x216, local copies, waits for them, and re-layouts  25.5 us
    all_to_all x1, waiting for transfers between devices, shards(): lax.all_to_all(solution, 'tm', split_axis=3, concat_axis=0, tiled=True)  24.7 us
    all_to_all x1, waiting for transfers between devices, shards(): lax.all_to_all(field, 'tm', split_axis=3, concat_axis=0, tiled=True)  24.6 us
    all_to_all x1, waiting for transfers between devices, shards(): lax.all_to_all(jnp.stack(jnp.split(spectral, lax.axis_size('tm'), axis=0)...  20.2 us
  transfers between devices with their start and end apart: 31, of which 4 were waited for; matrix products, arithmetic and copies ran while one was open for 15% of the time, Pallas kernels for 0%

profile of v1, /device:TPU:0, one launch (start us, length us, event | category | flops | bytes accessed | tf_op | source)
XLA Modules:
  0.0 401.4 jit_solution(11748597203675588995)
XLA Ops:
  2.4 5.7 %collective-permute-start.2 = (f32[4,256,128]{2,0,1:T(4,128)}, f32[4,256,128]{2,0,1:T(4,128)}, u32[]{:S(2)}, u32[]{:S(2)}) collective-permute-start(f32[4,256,128]{2,0,1:T(4,128)} %bitcast.144), channel_id=1, source_target_pairs={{0,8},{8,16},{16,24},{1,9},{9,17},{17,25},{2,10},{10,18},{18,26},{... | collective-permute-start | bytes 1572872 | tf_op jit(solution)/shard_map/ppermute | solution.py:28
  9.1 1.5 pad_maximum_fusion.12
  16.8 2.3 copy.99
  19.0 2.2 copy.100
  24.3 2.0 multiply_bitcast_fusion.1
  26.3 3.4 add_add_fusion
  30.2 1.6 copy-done.23
  31.8 3.9 fusion.37
  35.7 1.7 stack.91
  37.4 3.8 all-to-all-start
  41.6 24.6 %all-to-all-done = f32[2,2,4,256,128]{4,2,0,1,3:T(4,128)S(1)} async-done(((f32[2,2,4,256,128]{4,2,0,1,3:T(4,128)}), f32[2,2,4,256,128]{4,2,0,1,3:T(4,128)S(1)}, u32[]{:S(2)}, u32[]{:S(2)}) %all-to-all-start) | async-done | bytes 2097184 | tf_op jit(solution)/shard_map/all_to_all | solution.py:112
  66.2 2.0 copy.108
  68.2 1.7 reshape.231
  69.9 1.9 fusion.83
  72.3 1.5 pad_maximum_fusion.3
  73.8 3.7 all-to-all-start.1
  83.5 20.2 %all-to-all-done.1 = f32[4,2,2,4,64,128]{5,4,3,2,1,0:T(8,128)S(1)} async-done(((f32[4,2,2,4,64,128]{5,4,3,2,1,0:T(8,128)}), f32[4,2,2,4,64,128]{5,4,3,2,1,0:T(8,128)S(1)}, u32[]{:S(2)}, u32[]{:S(2)}) %all-to-all-start.1) | async-done | bytes 2097184 | tf_op jit(solution)/shard_map/all_to_all | solution.py:114
  103.9 1.9 multiply_subtract_fusion
  106.1 222.9 %while.17 = (s32[]{:T(128)}, f32[2,2,4,256,128]{4,3,2,1,0:T(8,128)S(1)}, f32[2,4,256,128]{3,2,1,0:T(8,128)}, f32[2,1,1,1]{0,3,2,1:T(1,128)S(1)}, f32[2,1,1,1]{0,...) while((s32[]{:T(128)}, ...), condition=%wide.region_1.2_spmd.clone.clone, body=%wide.region_0.1_spmd.clone.clone.sunk | while | flops 16252937 | bytes 94683824 | solution.py:163
  108.5 3.8 collective-permute-start.1
  112.4 2.4 fusion.94
  117.8 3.3 fusion.95
  125.0 5.9 %collective-permute-start.1 = (f32[2,2,1,256,128]{4,3,2,1,0:T(8,128)}, f32[2,2,1,256,128]{4,3,2,1,0:T(8,128)}, u32[]{:S(2)}, u32[]{:S(2)}) collective-permute-start(f32[2,2,1,256,128]{4,3,2,1,0:T(8,128)} %get-tuple-element.683), channel_id=1, source_target_pairs={{0,1},{1,2},{2,3},{3,4},{4,5},{5,6},{6,7},{8,9},{9,10},{10,11},{11... | collective-permute-start | bytes 1572872 | tf_op jit(solution)/shard_map/while/body/eval_jaxpr/ppermute | solution.py:17
  131.0 2.4 fusion.94
  136.4 3.3 fusion.95
  143.6 6.1 %collective-permute-start.1 = (f32[2,2,1,256,128]{4,3,2,1,0:T(8,128)}, f32[2,2,1,256,128]{4,3,2,1,0:T(8,128)}, u32[]{:S(2)}, u32[]{:S(2)}) collective-permute-start(f32[2,2,1,256,128]{4,3,2,1,0:T(8,128)} %get-tuple-element.683), channel_id=1, source_target_pairs={{0,1},{1,2},{2,3},{3,4},{4,5},{5,6},{6,7},{8,9},{9,10},{10,11},{11... | collective-permute-start | bytes 1572872 | tf_op jit(solution)/shard_map/while/body/eval_jaxpr/ppermute | solution.py:17
  149.8 2.4 fusion.94
  155.2 3.3 fusion.95
  162.4 6.1 %collective-permute-start.1 = (f32[2,2,1,256,128]{4,3,2,1,0:T(8,128)}, f32[2,2,1,256,128]{4,3,2,1,0:T(8,128)}, u32[]{:S(2)}, u32[]{:S(2)}) collective-permute-start(f32[2,2,1,256,128]{4,3,2,1,0:T(8,128)} %get-tuple-element.683), channel_id=1, source_target_pairs={{0,1},{1,2},{2,3},{3,4},{4,5},{5,6},{6,7},{8,9},{9,10},{10,11},{11... | collective-permute-start | bytes 1572872 | tf_op jit(solution)/shard_map/while/body/eval_jaxpr/ppermute | solution.py:17
  168.5 2.4 fusion.94
  173.9 3.3 fusion.95
  181.2 6.1 %collective-permute-start.1 = (f32[2,2,1,256,128]{4,3,2,1,0:T(8,128)}, f32[2,2,1,256,128]{4,3,2,1,0:T(8,128)}, u32[]{:S(2)}, u32[]{:S(2)}) collective-permute-start(f32[2,2,1,256,128]{4,3,2,1,0:T(8,128)} %get-tuple-element.683), channel_id=1, source_target_pairs={{0,1},{1,2},{2,3},{3,4},{4,5},{5,6},{6,7},{8,9},{9,10},{10,11},{11... | collective-permute-start | bytes 1572872 | tf_op jit(solution)/shard_map/while/body/eval_jaxpr/ppermute | solution.py:17
  187.3 2.4 fusion.94
  192.7 3.3 fusion.95
  200.0 6.1 %collective-permute-start.1 = (f32[2,2,1,256,128]{4,3,2,1,0:T(8,128)}, f32[2,2,1,256,128]{4,3,2,1,0:T(8,128)}, u32[]{:S(2)}, u32[]{:S(2)}) collective-permute-start(f32[2,2,1,256,128]{4,3,2,1,0:T(8,128)} %get-tuple-element.683), channel_id=1, source_target_pairs={{0,1},{1,2},{2,3},{3,4},{4,5},{5,6},{6,7},{8,9},{9,10},{10,11},{11... | collective-permute-start | bytes 1572872 | tf_op jit(solution)/shard_map/while/body/eval_jaxpr/ppermute | solution.py:17
  206.1 2.4 fusion.94
  211.5 3.3 fusion.95
  218.7 6.1 %collective-permute-start.1 = (f32[2,2,1,256,128]{4,3,2,1,0:T(8,128)}, f32[2,2,1,256,128]{4,3,2,1,0:T(8,128)}, u32[]{:S(2)}, u32[]{:S(2)}) collective-permute-start(f32[2,2,1,256,128]{4,3,2,1,0:T(8,128)} %get-tuple-element.683), channel_id=1, source_target_pairs={{0,1},{1,2},{2,3},{3,4},{4,5},{5,6},{6,7},{8,9},{9,10},{10,11},{11... | collective-permute-start | bytes 1572872 | tf_op jit(solution)/shard_map/while/body/eval_jaxpr/ppermute | solution.py:17
  224.9 2.4 fusion.94
  230.3 3.3 fusion.95
  237.5 6.1 %collective-permute-start.1 = (f32[2,2,1,256,128]{4,3,2,1,0:T(8,128)}, f32[2,2,1,256,128]{4,3,2,1,0:T(8,128)}, u32[]{:S(2)}, u32[]{:S(2)}) collective-permute-start(f32[2,2,1,256,128]{4,3,2,1,0:T(8,128)} %get-tuple-element.683), channel_id=1, source_target_pairs={{0,1},{1,2},{2,3},{3,4},{4,5},{5,6},{6,7},{8,9},{9,10},{10,11},{11... | collective-permute-start | bytes 1572872 | tf_op jit(solution)/shard_map/while/body/eval_jaxpr/ppermute | solution.py:17
  243.7 2.4 fusion.94
  249.1 3.3 fusion.95
  256.3 6.1 %collective-permute-start.1 = (f32[2,2,1,256,128]{4,3,2,1,0:T(8,128)}, f32[2,2,1,256,128]{4,3,2,1,0:T(8,128)}, u32[]{:S(2)}, u32[]{:S(2)}) collective-permute-start(f32[2,2,1,256,128]{4,3,2,1,0:T(8,128)} %get-tuple-element.683), channel_id=1, source_target_pairs={{0,1},{1,2},{2,3},{3,4},{4,5},{5,6},{6,7},{8,9},{9,10},{10,11},{11... | collective-permute-start | bytes 1572872 | tf_op jit(solution)/shard_map/while/body/eval_jaxpr/ppermute | solution.py:17
  262.4 2.4 fusion.94
  267.8 3.3 fusion.95
  275.1 6.1 %collective-permute-start.1 = (f32[2,2,1,256,128]{4,3,2,1,0:T(8,128)}, f32[2,2,1,256,128]{4,3,2,1,0:T(8,128)}, u32[]{:S(2)}, u32[]{:S(2)}) collective-permute-start(f32[2,2,1,256,128]{4,3,2,1,0:T(8,128)} %get-tuple-element.683), channel_id=1, source_target_pairs={{0,1},{1,2},{2,3},{3,4},{4,5},{5,6},{6,7},{8,9},{9,10},{10,11},{11... | collective-permute-start | bytes 1572872 | tf_op jit(solution)/shard_map/while/body/eval_jaxpr/ppermute | solution.py:17
  281.2 2.4 fusion.94
  286.6 3.3 fusion.95
  293.9 6.1 %collective-permute-start.1 = (f32[2,2,1,256,128]{4,3,2,1,0:T(8,128)}, f32[2,2,1,256,128]{4,3,2,1,0:T(8,128)}, u32[]{:S(2)}, u32[]{:S(2)}) collective-permute-start(f32[2,2,1,256,128]{4,3,2,1,0:T(8,128)} %get-tuple-element.683), channel_id=1, source_target_pairs={{0,1},{1,2},{2,3},{3,4},{4,5},{5,6},{6,7},{8,9},{9,10},{10,11},{11... | collective-permute-start | bytes 1572872 | tf_op jit(solution)/shard_map/while/body/eval_jaxpr/ppermute | solution.py:17
  300.0 2.4 fusion.94
  305.4 3.3 fusion.95
  312.6 6.1 %collective-permute-start.1 = (f32[2,2,1,256,128]{4,3,2,1,0:T(8,128)}, f32[2,2,1,256,128]{4,3,2,1,0:T(8,128)}, u32[]{:S(2)}, u32[]{:S(2)}) collective-permute-start(f32[2,2,1,256,128]{4,3,2,1,0:T(8,128)} %get-tuple-element.683), channel_id=1, source_target_pairs={{0,1},{1,2},{2,3},{3,4},{4,5},{5,6},{6,7},{8,9},{9,10},{10,11},{11... | collective-permute-start | bytes 1572872 | tf_op jit(solution)/shard_map/while/body/eval_jaxpr/ppermute | solution.py:17
  318.8 2.4 fusion.94
  324.2 3.3 fusion.95
  329.0 2.7 copy.66
  331.7 3.8 all-to-all-start.2
  335.9 24.7 %all-to-all-done.2 = f32[2,2,4,256,128]{4,2,1,0,3:T(4,128)S(1)} async-done(((f32[2,2,4,256,128]{4,2,1,0,3:T(4,128)}), f32[2,2,4,256,128]{4,2,1,0,3:T(4,128)S(1)}, u32[]{:S(2)}, u32[]{:S(2)}) %all-to-all-start.2) | async-done | bytes 2097184 | tf_op jit(solution)/shard_map/all_to_all | solution.py:164
  360.6 2.0 copy.107
  362.5 1.7 reshape.236
  364.7 2.8 fusion.28
  367.5 1.7 copy.69
  369.3 3.6 all-to-all-start.3
  372.9 26.1 %all-to-all-done.3 = f32[8,2,4,64,128]{4,3,2,1,0:T(8,128)S(1)} async-done(((f32[8,2,4,64,128]{4,3,2,1,0:T(8,128)}), f32[8,2,4,64,128]{4,3,2,1,0:T(8,128)S(1)}, u32[]{:S(2)}, u32[]{:S(2)}) %all-to-all-start.3) | async-done | bytes 2097184 | tf_op jit(solution)/shard_map/all_to_all | solution.py:165
  (412 shorter events, 103.6 us)
Async XLA Ops:
  0.0 77.8 %copy-start = (f32[8]{0:T(128)S(1)}, f32[8]{0:T(128)}, u32[]{:S(2)}) copy-start(f32[8]{0:T(128)} %param.13) | copy-start | bytes 100
  0.0 8.0 %copy-start.12 = (f32[2,4,256,128]{3,2,1,0:T(8,128)S(1)}, f32[2,4,256,128]{3,2,1,0:T(8,128)}, u32[]{:S(2)}) copy-start(f32[2,4,256,128]{3,2,1,0:T(8,128)} %param.8) | copy-start | bytes 3145732
  0.0 8.7 %copy-start.6 = (f32[4,256,128]{2,1,0:T(8,128)S(1)}, f32[4,256,128]{2,1,0:T(8,128)}, u32[]{:S(2)}) copy-start(f32[4,256,128]{2,1,0:T(8,128)} %param.10) | copy-start | bytes 1572868
  2.4 27.4 %collective-permute-start.2 = (f32[4,256,128]{2,0,1:T(4,128)}, f32[4,256,128]{2,0,1:T(4,128)}, u32[]{:S(2)}, u32[]{:S(2)}) collective-permute-start(f32[4,256,128]{2,0,1:T(4,128)} %bitcast.144), channel_id=1, source_target_pairs={{0,8},{8,16},{16,24},{1,9},{9,17},{17,25},{2,10},{10,18},{18,26},{... | collective-permute-start | bytes 1572872 | tf_op jit(solution)/shard_map/ppermute | solution.py:28
  10.6 13.7 %collective-permute-start.3 = (f32[3,1,256,128]{3,1,0,2:T(1,128)}, f32[3,1,256,128]{3,1,0,2:T(1,128)S(1)}, u32[]{:S(2)}, u32[]{:S(2)}) collective-permute-start(f32[3,1,256,128]{3,1,0,2:T(1,128)} %get-tuple-element.554), channel_id=1, source_target_pairs={{0,1},{1,2},{2,3},{3,4},{4,5},{5,6},{6,7},{8,9},{9,10},{10,11},{11... | collective-permute-start | bytes 1179656 | tf_op jit(solution)/shard_map/ppermute | solution.py:17
  12.1 12.2 %collective-permute-start.4 = (f32[3,1,256,128]{3,1,0,2:T(1,128)}, f32[3,1,256,128]{3,1,0,2:T(1,128)}, u32[]{:S(2)}, u32[]{:S(2)}) collective-permute-start(f32[3,1,256,128]{3,1,0,2:T(1,128)} %get-tuple-element.555), channel_id=1, source_target_pairs={{1,0},{2,1},{3,2},{4,3},{5,4},{6,5},{7,6},{9,8},{10,9},{11,10},{12... | collective-permute-start | bytes 1179656 | tf_op jit(solution)/shard_map/ppermute | solution.py:20
  16.8 4.4 %copy-start.29 = (f32[4,256,127]{2,1,0:T(8,128)S(1)}, f32[4,256,127]{2,1,0:T(8,128)}, u32[]{:S(2)}) copy-start(f32[4,256,127]{2,1,0:T(8,128)} %get-tuple-element.561) | copy-start | bytes 1560580
  16.8 5.6 %copy-start.28 = (f32[4,256,127]{2,1,0:T(8,128)S(1)}, f32[4,256,127]{2,1,0:T(8,128)}, u32[]{:S(2)}) copy-start(f32[4,256,127]{2,1,0:T(8,128)} %get-tuple-element.562) | copy-start | bytes 1560580
  26.3 3.5 copy-start.32
  26.3 3.9 copy-start.33
  29.7 5.9 %copy-start.14 = (f32[4,256,128]{2,0,1:T(4,128)}, f32[4,256,128]{2,0,1:T(4,128)S(1)}, u32[]{:S(2)}) copy-start(f32[4,256,128]{2,0,1:T(4,128)S(1)} %get-tuple-element.537) | copy-start | bytes 1572868
  29.7 6.0 %copy-start.16 = (f32[4,256,128]{2,0,1:T(4,128)}, f32[4,256,128]{2,0,1:T(4,128)S(1)}, u32[]{:S(2)}) copy-start(f32[4,256,128]{2,0,1:T(4,128)S(1)} %get-tuple-element.536) | copy-start | bytes 1572868
  29.7 6.0 %copy-start.18 = (f32[4,256,128]{2,0,1:T(4,128)}, f32[4,256,128]{2,0,1:T(4,128)S(1)}, u32[]{:S(2)}) copy-start(f32[4,256,128]{2,0,1:T(4,128)S(1)} %get-tuple-element.535) | copy-start | bytes 1572868
  29.7 6.0 %copy-start.20 = (f32[4,256,128]{2,0,1:T(4,128)}, f32[4,256,128]{2,0,1:T(4,128)S(1)}, u32[]{:S(2)}) copy-start(f32[4,256,128]{2,0,1:T(4,128)S(1)} %get-tuple-element.534) | copy-start | bytes 1572868
  29.7 6.0 %copy-start.21 = (f32[4,256,128]{2,0,1:T(4,128)}, f32[4,256,128]{2,0,1:T(4,128)S(1)}, u32[]{:S(2)}) copy-start(f32[4,256,128]{2,0,1:T(4,128)S(1)} %get-tuple-element.531) | copy-start | bytes 1572868
  37.4 28.8 %all-to-all-start = ((f32[2,2,4,256,128]{4,2,0,1,3:T(4,128)}), f32[2,2,4,256,128]{4,2,0,1,3:T(4,128)S(1)}, u32[]{:S(2)}, u32[]{:S(2)}) async-start(f32[2,2,4,256,128]{4,2,0,1,3:T(4,128)} %stack.91), calls=%async_computation | async-start | bytes 4194304 | tf_op jit(solution)/shard_map/all_to_all | solution.py:112
  73.8 3.8 copy-start.34
  73.8 4.2 %copy-start.22 = (f32[4,256,128]{2,0,1:T(4,128)S(1)}, f32[4,256,128]{2,0,1:T(4,128)}, u32[]{:S(2)}) copy-start(f32[4,256,128]{2,0,1:T(4,128)} %copy-done.21) | copy-start | bytes 1572868
  73.8 29.9 %all-to-all-start.1 = ((f32[4,2,2,4,64,128]{5,4,3,2,1,0:T(8,128)}), f32[4,2,2,4,64,128]{5,4,3,2,1,0:T(8,128)S(1)}, u32[]{:S(2)}, u32[]{:S(2)}) async-start(f32[4,2,2,4,64,128]{5,4,3,2,1,0:T(8,128)} %pad_maximum_fusion.3), calls=%async_computation.1 | async-start | bytes 4194304 | tf_op jit(solution)/shard_map/all_to_all | solution.py:114
  78.0 3.7 copy-start.25
  79.2 3.4 copy-start.24
  107.3 8.4 %collective-permute-start = (f32[2,2,1,256,128]{4,3,2,1,0:T(8,128)}, f32[2,2,1,256,128]{4,3,2,1,0:T(8,128)}, u32[]{:S(2)}, u32[]{:S(2)}) collective-permute-start(f32[2,2,1,256,128]{4,3,2,1,0:T(8,128)} %get-tuple-element.682), channel_id=1, source_target_pairs={{1,0},{2,1},{3,2},{4,3},{5,4},{6,5},{7,6},{9,8},{10,9},{11,10},{12... | collective-permute-start | bytes 1572872 | tf_op jit(solution)/shard_map/while/body/eval_jaxpr/ppermute | solution.py:20
  108.5 7.1 %collective-permute-start.1 = (f32[2,2,1,256,128]{4,3,2,1,0:T(8,128)}, f32[2,2,1,256,128]{4,3,2,1,0:T(8,128)}, u32[]{:S(2)}, u32[]{:S(2)}) collective-permute-start(f32[2,2,1,256,128]{4,3,2,1,0:T(8,128)} %get-tuple-element.683), channel_id=1, source_target_pairs={{0,1},{1,2},{2,3},{3,4},{4,5},{5,6},{6,7},{8,9},{9,10},{10,11},{11... | collective-permute-start | bytes 1572872 | tf_op jit(solution)/shard_map/while/body/eval_jaxpr/ppermute | solution.py:17
  117.8 3.4 copy-start.4
  117.8 3.4 copy-start.5
  123.7 10.5 %collective-permute-start = (f32[2,2,1,256,128]{4,3,2,1,0:T(8,128)}, f32[2,2,1,256,128]{4,3,2,1,0:T(8,128)}, u32[]{:S(2)}, u32[]{:S(2)}) collective-permute-start(f32[2,2,1,256,128]{4,3,2,1,0:T(8,128)} %get-tuple-element.682), channel_id=1, source_target_pairs={{1,0},{2,1},{3,2},{4,3},{5,4},{6,5},{7,6},{9,8},{10,9},{11,10},{12... | collective-permute-start | bytes 1572872 | tf_op jit(solution)/shard_map/while/body/eval_jaxpr/ppermute | solution.py:20
  125.0 9.2 %collective-permute-start.1 = (f32[2,2,1,256,128]{4,3,2,1,0:T(8,128)}, f32[2,2,1,256,128]{4,3,2,1,0:T(8,128)}, u32[]{:S(2)}, u32[]{:S(2)}) collective-permute-start(f32[2,2,1,256,128]{4,3,2,1,0:T(8,128)} %get-tuple-element.683), channel_id=1, source_target_pairs={{0,1},{1,2},{2,3},{3,4},{4,5},{5,6},{6,7},{8,9},{9,10},{10,11},{11... | collective-permute-start | bytes 1572872 | tf_op jit(solution)/shard_map/while/body/eval_jaxpr/ppermute | solution.py:17
  136.4 3.4 copy-start.4
  136.4 3.4 copy-start.5
  142.3 10.7 %collective-permute-start = (f32[2,2,1,256,128]{4,3,2,1,0:T(8,128)}, f32[2,2,1,256,128]{4,3,2,1,0:T(8,128)}, u32[]{:S(2)}, u32[]{:S(2)}) collective-permute-start(f32[2,2,1,256,128]{4,3,2,1,0:T(8,128)} %get-tuple-element.682), channel_id=1, source_target_pairs={{1,0},{2,1},{3,2},{4,3},{5,4},{6,5},{7,6},{9,8},{10,9},{11,10},{12... | collective-permute-start | bytes 1572872 | tf_op jit(solution)/shard_map/while/body/eval_jaxpr/ppermute | solution.py:20
  143.6 9.4 %collective-permute-start.1 = (f32[2,2,1,256,128]{4,3,2,1,0:T(8,128)}, f32[2,2,1,256,128]{4,3,2,1,0:T(8,128)}, u32[]{:S(2)}, u32[]{:S(2)}) collective-permute-start(f32[2,2,1,256,128]{4,3,2,1,0:T(8,128)} %get-tuple-element.683), channel_id=1, source_target_pairs={{0,1},{1,2},{2,3},{3,4},{4,5},{5,6},{6,7},{8,9},{9,10},{10,11},{11... | collective-permute-start | bytes 1572872 | tf_op jit(solution)/shard_map/while/body/eval_jaxpr/ppermute | solution.py:17
  155.2 3.4 copy-start.5
  161.1 10.7 %collective-permute-start = (f32[2,2,1,256,128]{4,3,2,1,0:T(8,128)}, f32[2,2,1,256,128]{4,3,2,1,0:T(8,128)}, u32[]{:S(2)}, u32[]{:S(2)}) collective-permute-start(f32[2,2,1,256,128]{4,3,2,1,0:T(8,128)} %get-tuple-element.682), channel_id=1, source_target_pairs={{1,0},{2,1},{3,2},{4,3},{5,4},{6,5},{7,6},{9,8},{10,9},{11,10},{12... | collective-permute-start | bytes 1572872 | tf_op jit(solution)/shard_map/while/body/eval_jaxpr/ppermute | solution.py:20
  162.4 9.4 %collective-permute-start.1 = (f32[2,2,1,256,128]{4,3,2,1,0:T(8,128)}, f32[2,2,1,256,128]{4,3,2,1,0:T(8,128)}, u32[]{:S(2)}, u32[]{:S(2)}) collective-permute-start(f32[2,2,1,256,128]{4,3,2,1,0:T(8,128)} %get-tuple-element.683), channel_id=1, source_target_pairs={{0,1},{1,2},{2,3},{3,4},{4,5},{5,6},{6,7},{8,9},{9,10},{10,11},{11... | collective-permute-start | bytes 1572872 | tf_op jit(solution)/shard_map/while/body/eval_jaxpr/ppermute | solution.py:17
  173.9 3.4 copy-start.4
  173.9 3.4 copy-start.5
  179.9 10.7 %collective-permute-start = (f32[2,2,1,256,128]{4,3,2,1,0:T(8,128)}, f32[2,2,1,256,128]{4,3,2,1,0:T(8,128)}, u32[]{:S(2)}, u32[]{:S(2)}) collective-permute-start(f32[2,2,1,256,128]{4,3,2,1,0:T(8,128)} %get-tuple-element.682), channel_id=1, source_target_pairs={{1,0},{2,1},{3,2},{4,3},{5,4},{6,5},{7,6},{9,8},{10,9},{11,10},{12... | collective-permute-start | bytes 1572872 | tf_op jit(solution)/shard_map/while/body/eval_jaxpr/ppermute | solution.py:20
  181.2 9.4 %collective-permute-start.1 = (f32[2,2,1,256,128]{4,3,2,1,0:T(8,128)}, f32[2,2,1,256,128]{4,3,2,1,0:T(8,128)}, u32[]{:S(2)}, u32[]{:S(2)}) collective-permute-start(f32[2,2,1,256,128]{4,3,2,1,0:T(8,128)} %get-tuple-element.683), channel_id=1, source_target_pairs={{0,1},{1,2},{2,3},{3,4},{4,5},{5,6},{6,7},{8,9},{9,10},{10,11},{11... | collective-permute-start | bytes 1572872 | tf_op jit(solution)/shard_map/while/body/eval_jaxpr/ppermute | solution.py:17
  192.7 3.4 copy-start.4
  192.7 3.4 copy-start.5
  198.7 10.7 %collective-permute-start = (f32[2,2,1,256,128]{4,3,2,1,0:T(8,128)}, f32[2,2,1,256,128]{4,3,2,1,0:T(8,128)}, u32[]{:S(2)}, u32[]{:S(2)}) collective-permute-start(f32[2,2,1,256,128]{4,3,2,1,0:T(8,128)} %get-tuple-element.682), channel_id=1, source_target_pairs={{1,0},{2,1},{3,2},{4,3},{5,4},{6,5},{7,6},{9,8},{10,9},{11,10},{12... | collective-permute-start | bytes 1572872 | tf_op jit(solution)/shard_map/while/body/eval_jaxpr/ppermute | solution.py:20
  200.0 9.4 %collective-permute-start.1 = (f32[2,2,1,256,128]{4,3,2,1,0:T(8,128)}, f32[2,2,1,256,128]{4,3,2,1,0:T(8,128)}, u32[]{:S(2)}, u32[]{:S(2)}) collective-permute-start(f32[2,2,1,256,128]{4,3,2,1,0:T(8,128)} %get-tuple-element.683), channel_id=1, source_target_pairs={{0,1},{1,2},{2,3},{3,4},{4,5},{5,6},{6,7},{8,9},{9,10},{10,11},{11... | collective-permute-start | bytes 1572872 | tf_op jit(solution)/shard_map/while/body/eval_jaxpr/ppermute | solution.py:17
  211.5 3.4 copy-start.5
  217.5 10.7 %collective-permute-start = (f32[2,2,1,256,128]{4,3,2,1,0:T(8,128)}, f32[2,2,1,256,128]{4,3,2,1,0:T(8,128)}, u32[]{:S(2)}, u32[]{:S(2)}) collective-permute-start(f32[2,2,1,256,128]{4,3,2,1,0:T(8,128)} %get-tuple-element.682), channel_id=1, source_target_pairs={{1,0},{2,1},{3,2},{4,3},{5,4},{6,5},{7,6},{9,8},{10,9},{11,10},{12... | collective-permute-start | bytes 1572872 | tf_op jit(solution)/shard_map/while/body/eval_jaxpr/ppermute | solution.py:20
  218.7 9.4 %collective-permute-start.1 = (f32[2,2,1,256,128]{4,3,2,1,0:T(8,128)}, f32[2,2,1,256,128]{4,3,2,1,0:T(8,128)}, u32[]{:S(2)}, u32[]{:S(2)}) collective-permute-start(f32[2,2,1,256,128]{4,3,2,1,0:T(8,128)} %get-tuple-element.683), channel_id=1, source_target_pairs={{0,1},{1,2},{2,3},{3,4},{4,5},{5,6},{6,7},{8,9},{9,10},{10,11},{11... | collective-permute-start | bytes 1572872 | tf_op jit(solution)/shard_map/while/body/eval_jaxpr/ppermute | solution.py:17
  230.3 3.4 copy-start.4
  230.3 3.4 copy-start.5
  236.2 10.7 %collective-permute-start = (f32[2,2,1,256,128]{4,3,2,1,0:T(8,128)}, f32[2,2,1,256,128]{4,3,2,1,0:T(8,128)}, u32[]{:S(2)}, u32[]{:S(2)}) collective-permute-start(f32[2,2,1,256,128]{4,3,2,1,0:T(8,128)} %get-tuple-element.682), channel_id=1, source_target_pairs={{1,0},{2,1},{3,2},{4,3},{5,4},{6,5},{7,6},{9,8},{10,9},{11,10},{12... | collective-permute-start | bytes 1572872 | tf_op jit(solution)/shard_map/while/body/eval_jaxpr/ppermute | solution.py:20
  237.5 9.4 %collective-permute-start.1 = (f32[2,2,1,256,128]{4,3,2,1,0:T(8,128)}, f32[2,2,1,256,128]{4,3,2,1,0:T(8,128)}, u32[]{:S(2)}, u32[]{:S(2)}) collective-permute-start(f32[2,2,1,256,128]{4,3,2,1,0:T(8,128)} %get-tuple-element.683), channel_id=1, source_target_pairs={{0,1},{1,2},{2,3},{3,4},{4,5},{5,6},{6,7},{8,9},{9,10},{10,11},{11... | collective-permute-start | bytes 1572872 | tf_op jit(solution)/shard_map/while/body/eval_jaxpr/ppermute | solution.py:17
  249.1 3.4 copy-start.5
  255.0 10.7 %collective-permute-start = (f32[2,2,1,256,128]{4,3,2,1,0:T(8,128)}, f32[2,2,1,256,128]{4,3,2,1,0:T(8,128)}, u32[]{:S(2)}, u32[]{:S(2)}) collective-permute-start(f32[2,2,1,256,128]{4,3,2,1,0:T(8,128)} %get-tuple-element.682), channel_id=1, source_target_pairs={{1,0},{2,1},{3,2},{4,3},{5,4},{6,5},{7,6},{9,8},{10,9},{11,10},{12... | collective-permute-start | bytes 1572872 | tf_op jit(solution)/shard_map/while/body/eval_jaxpr/ppermute | solution.py:20
  256.3 9.4 %collective-permute-start.1 = (f32[2,2,1,256,128]{4,3,2,1,0:T(8,128)}, f32[2,2,1,256,128]{4,3,2,1,0:T(8,128)}, u32[]{:S(2)}, u32[]{:S(2)}) collective-permute-start(f32[2,2,1,256,128]{4,3,2,1,0:T(8,128)} %get-tuple-element.683), channel_id=1, source_target_pairs={{0,1},{1,2},{2,3},{3,4},{4,5},{5,6},{6,7},{8,9},{9,10},{10,11},{11... | collective-permute-start | bytes 1572872 | tf_op jit(solution)/shard_map/while/body/eval_jaxpr/ppermute | solution.py:17
  267.8 3.4 copy-start.5
  273.8 10.7 %collective-permute-start = (f32[2,2,1,256,128]{4,3,2,1,0:T(8,128)}, f32[2,2,1,256,128]{4,3,2,1,0:T(8,128)}, u32[]{:S(2)}, u32[]{:S(2)}) collective-permute-start(f32[2,2,1,256,128]{4,3,2,1,0:T(8,128)} %get-tuple-element.682), channel_id=1, source_target_pairs={{1,0},{2,1},{3,2},{4,3},{5,4},{6,5},{7,6},{9,8},{10,9},{11,10},{12... | collective-permute-start | bytes 1572872 | tf_op jit(solution)/shard_map/while/body/eval_jaxpr/ppermute | solution.py:20
  275.1 9.4 %collective-permute-start.1 = (f32[2,2,1,256,128]{4,3,2,1,0:T(8,128)}, f32[2,2,1,256,128]{4,3,2,1,0:T(8,128)}, u32[]{:S(2)}, u32[]{:S(2)}) collective-permute-start(f32[2,2,1,256,128]{4,3,2,1,0:T(8,128)} %get-tuple-element.683), channel_id=1, source_target_pairs={{0,1},{1,2},{2,3},{3,4},{4,5},{5,6},{6,7},{8,9},{9,10},{10,11},{11... | collective-permute-start | bytes 1572872 | tf_op jit(solution)/shard_map/while/body/eval_jaxpr/ppermute | solution.py:17
  286.6 3.4 copy-start.5
  292.6 10.7 %collective-permute-start = (f32[2,2,1,256,128]{4,3,2,1,0:T(8,128)}, f32[2,2,1,256,128]{4,3,2,1,0:T(8,128)}, u32[]{:S(2)}, u32[]{:S(2)}) collective-permute-start(f32[2,2,1,256,128]{4,3,2,1,0:T(8,128)} %get-tuple-element.682), channel_id=1, source_target_pairs={{1,0},{2,1},{3,2},{4,3},{5,4},{6,5},{7,6},{9,8},{10,9},{11,10},{12... | collective-permute-start | bytes 1572872 | tf_op jit(solution)/shard_map/while/body/eval_jaxpr/ppermute | solution.py:20
  293.9 9.4 %collective-permute-start.1 = (f32[2,2,1,256,128]{4,3,2,1,0:T(8,128)}, f32[2,2,1,256,128]{4,3,2,1,0:T(8,128)}, u32[]{:S(2)}, u32[]{:S(2)}) collective-permute-start(f32[2,2,1,256,128]{4,3,2,1,0:T(8,128)} %get-tuple-element.683), channel_id=1, source_target_pairs={{0,1},{1,2},{2,3},{3,4},{4,5},{5,6},{6,7},{8,9},{9,10},{10,11},{11... | collective-permute-start | bytes 1572872 | tf_op jit(solution)/shard_map/while/body/eval_jaxpr/ppermute | solution.py:17
  305.4 3.4 copy-start.5
  311.4 10.7 %collective-permute-start = (f32[2,2,1,256,128]{4,3,2,1,0:T(8,128)}, f32[2,2,1,256,128]{4,3,2,1,0:T(8,128)}, u32[]{:S(2)}, u32[]{:S(2)}) collective-permute-start(f32[2,2,1,256,128]{4,3,2,1,0:T(8,128)} %get-tuple-element.682), channel_id=1, source_target_pairs={{1,0},{2,1},{3,2},{4,3},{5,4},{6,5},{7,6},{9,8},{10,9},{11,10},{12... | collective-permute-start | bytes 1572872 | tf_op jit(solution)/shard_map/while/body/eval_jaxpr/ppermute | solution.py:20
  312.6 9.4 %collective-permute-start.1 = (f32[2,2,1,256,128]{4,3,2,1,0:T(8,128)}, f32[2,2,1,256,128]{4,3,2,1,0:T(8,128)}, u32[]{:S(2)}, u32[]{:S(2)}) collective-permute-start(f32[2,2,1,256,128]{4,3,2,1,0:T(8,128)} %get-tuple-element.683), channel_id=1, source_target_pairs={{0,1},{1,2},{2,3},{3,4},{4,5},{5,6},{6,7},{8,9},{9,10},{10,11},{11... | collective-permute-start | bytes 1572872 | tf_op jit(solution)/shard_map/while/body/eval_jaxpr/ppermute | solution.py:17
  324.2 3.4 copy-start.5
  331.7 28.8 %all-to-all-start.2 = ((f32[2,2,4,256,128]{4,2,1,0,3:T(4,128)}), f32[2,2,4,256,128]{4,2,1,0,3:T(4,128)S(1)}, u32[]{:S(2)}, u32[]{:S(2)}) async-start(f32[2,2,4,256,128]{4,2,1,0,3:T(4,128)} %copy.66), calls=%async_computation.2 | async-start | bytes 4194304 | tf_op jit(solution)/shard_map/all_to_all | solution.py:164
  369.3 29.8 %all-to-all-start.3 = ((f32[8,2,4,64,128]{4,3,2,1,0:T(8,128)}), f32[8,2,4,64,128]{4,3,2,1,0:T(8,128)S(1)}, u32[]{:S(2)}, u32[]{:S(2)}) async-start(f32[8,2,4,64,128]{4,3,2,1,0:T(8,128)} %copy.69), calls=%async_computation.3 | async-start | bytes 4194304 | tf_op jit(solution)/shard_map/all_to_all | solution.py:165
  (101 other events, 244.5 us)
